TPU v7x, 32 devices: a whole 2x2x4 slice. The times are simulated.
32 devices in a mesh: grp: 2 (over x), tm: 4 (over y, core), tile: 4 (over z).
Axes of the slice: x: 2, y: 2, z: 4, core: 2. Of those that a mesh axis runs over, the one named last changes fastest.
Arguments:
- frames: bfloat16 [64, 1024, 1024], P(('grp', 'tm'), 'tile'), parts along dimension 0, may hold values from -3 to 3
- inverse_taps: float32 [48], replicated, may hold values from -3 to 3
- mode_rate: float32 [1024, 1024], P(None, 'tile'), may hold values from 0.00625 to 0.2
- frame_factor: float32 [64], P(('grp', 'tm')), parts along dimension 0, may hold values from 0.5 to 1
Outputs:
- superheat: bfloat16 [64, 1024, 1024], P(('grp', 'tm'), 'tile'), parts along dimension 0
There are 2 independent parts, one for each index of `grp`. A program takes and returns all parts, laid end to end along the dimension named above; an argument that names none is the same for every part. Nothing has to cross between parts.
All inputs are finite; a program needn't handle non-finite values.
Results may differ from a plain program's by a relative error of at most 0.0097.
Values may be sent and summed in bfloat16 or wider, within the bound.
A program may use at most 128 MiB of HBM per device.

v0:
```python
import jax
import jax.numpy as jnp
from jax import lax
from jax.sharding import PartitionSpec as P


def from_behind(block, axis, distance):
    devices = range(lax.axis_size(axis))
    route = [(i - distance, i) for i in devices if i - distance in devices]
    return lax.ppermute(block, axis, route)


def cosine_matrix(points):
    freq_idx = jnp.arange(points, dtype=jnp.int32)[:, None]
    cell_idx = jnp.arange(points, dtype=jnp.int32)[None, :]
    phase = (2 * cell_idx + 1) * freq_idx % (4 * points)
    angle = jnp.pi * phase.astype(jnp.float32) / (2.0 * points)
    values = jnp.cos(angle) * jnp.sqrt(2.0 / points)
    values = jnp.where(freq_idx == 0, values / jnp.sqrt(2.0), values)
    return values.astype(jnp.bfloat16)


def on_device(frames, inverse_taps, mode_rate, frame_factor):
    segment_span, tile_rows, frame_side = frames.shape
    tap_count = inverse_taps.shape[0]
    basis = cosine_matrix(frame_side)
    taps_b = inverse_taps.astype(jnp.bfloat16).astype(jnp.float32)
    offset = (
        jnp.arange(segment_span)[:, None]
        + (tap_count - 1)
        - jnp.arange(segment_span + tap_count - 1)[None, :]
    )
    onehot = offset[:, :, None] == jnp.arange(tap_count)[None, None, :]
    toeplitz = jnp.sum(jnp.where(onehot, taps_b[None, None, :], 0.0), axis=2).astype(jnp.bfloat16)
    reach = (tap_count - 1 + segment_span - 1) // segment_span
    hop_count = min(reach, lax.axis_size("tm") - 1)
    received = []
    moving = frames
    for hop_index in range(hop_count):
        moving = from_behind(moving, "tm", 1)
        received.append(moving)
    missing = reach - hop_count
    pieces = []
    if missing > 0:
        pieces.append(jnp.zeros((missing * segment_span, tile_rows, frame_side), jnp.bfloat16))
    pieces = pieces + received[::-1]
    history_all = jnp.concatenate(pieces, axis=0)
    earlier = history_all[history_all.shape[0] - (tap_count - 1) :]
    joined = jnp.concatenate([earlier, frames], axis=0)
    wall_heat_flux = jnp.einsum("tj,jrw->trw", toeplitz, joined, preferred_element_type=jnp.float32)
    wall_heat_flux = wall_heat_flux.astype(jnp.bfloat16)
    spectra = jnp.einsum(
        "kr,frc->fkc",
        basis,
        lax.all_to_all(
            jnp.einsum(
                "frw,kw->frk", wall_heat_flux, basis, preferred_element_type=jnp.float32
            ).astype(jnp.bfloat16),
            "tile",
            split_axis=2,
            concat_axis=1,
            tiled=True,
        ),
        preferred_element_type=jnp.float32,
    )
    retain = jnp.exp(-mode_rate)

    def advance(held, inputs):
        decay, running = held
        spectrum, factor = inputs
        rate_now = retain * factor
        decay = rate_now * decay
        running = rate_now * running + spectrum
        return ((decay, running), (decay, running))

    start_decay = jnp.ones_like(retain)
    start_state = jnp.zeros_like(retain)
    (last_decay, last_state), (decays, partial_value) = lax.scan(
        advance, (start_decay, start_state), (spectra, frame_factor)
    )

    def turn(round_number, incoming):
        return from_behind(last_decay * incoming + last_state, "tm", 1)

    carried = lax.fori_loop(0, lax.axis_size("tm") - 1, turn, start_state)
    running_b = (partial_value + decays * carried[None]).astype(jnp.bfloat16)
    return jnp.einsum(
        "frk,kw->frw",
        lax.all_to_all(
            jnp.einsum("kr,fkc->frc", basis, running_b, preferred_element_type=jnp.float32).astype(
                jnp.bfloat16
            ),
            "tile",
            split_axis=1,
            concat_axis=2,
            tiled=True,
        ),
        basis,
        preferred_element_type=jnp.float32,
    ).astype(jnp.bfloat16)


def solution(mesh):
    return jax.shard_map(
        on_device,
        mesh=mesh,
        in_specs=(P(("grp", "tm"), "tile", None), P(), P(None, "tile"), P(("grp", "tm"))),
        out_specs=P(("grp", "tm"), "tile", None),
        check_vma=False,
    )
```

profile of v0, /device:TPU:1, one launch (start us, length us, event | category | flops | bytes accessed | tf_op | source)
XLA Modules:
  0.0 596.6 jit_solution(18411087734227628912)
XLA Ops:
  4.5 4.5 collective-permute-start.1
  9.1 45.4 %collective-permute-done.1 = bf16[8,256,1024]{2,0,1:T(8,128)(2,1)S(1)} collective-permute-done((bf16[8,256,1024]{2,0,1:T(8,128)(2,1)S(1)}, bf16[8,256,1024]{2,0,1:T(8,128)(2,1)S(1)}, u32[]{:S(2)}, u32[]{:S(2)}) %collective-permute-start.1) | collective-permute-done | bytes 4194336 | tf_op jit(solution)/shard_map/ppermute | solution.py:10
  58.9 45.4 %collective-permute-done.2 = bf16[8,256,1024]{2,0,1:T(8,128)(2,1)S(1)} collective-permute-done((bf16[8,256,1024]{2,0,1:T(8,128)(2,1)S(1)}, bf16[8,256,1024]{2,0,1:T(8,128)(2,1)S(1)}, u32[]{:S(2)}, u32[]{:S(2)}) %collective-permute-start.2) | collective-permute-done | bytes 4194336 | tf_op jit(solution)/shard_map/ppermute | solution.py:10
  109.0 45.1 %collective-permute-done.3 = bf16[8,256,1024]{2,0,1:T(8,128)(2,1)S(1)} collective-permute-done((bf16[8,256,1024]{2,0,1:T(8,128)(2,1)S(1)}, bf16[8,256,1024]{2,0,1:T(8,128)(2,1)S(1)}, u32[]{:S(2)}, u32[]{:S(2)}) %collective-permute-start.3) | collective-permute-done | bytes 4194336 | tf_op jit(solution)/shard_map/ppermute | solution.py:10
  154.1 14.9 %pad_maximum_fusion = bf16[47,256,1024]{2,0,1:T(8,128)(2,1)} fusion(bf16[8,256,1024]{2,0,1:T(8,128)(2,1)S(1)} %collective-permute-done.1, bf16[8,256,1024]{2,0,1:T(8,128)(2,1)S(1)} %collective-permute-done.2, bf16[8,256,1024]{2,0,1:T(8,128)(2,1)S(1)} %collective-permute-done.3, bf16[47]{0:T(256)(128)(2,1)S(1)} %pad_slice_fusion), kind=kLoop, calls=%fused_computation.11 | loop fusion | flops 98566144 | bytes 37224544 | tf_op jit(solution)/shard_map/concatenate | solution.py:47
  169.0 14.9 %fusion.18 = bf16[8,256,1024]{2,0,1:T(8,128)(2,1)} fusion(bf16[8,256,1024]{2,0,1:T(8,128)(2,1)} %copy-done, bf16[47,256,1024]{2,0,1:T(8,128)(2,1)} %pad_maximum_fusion, bf16[8,55]{1,0:T(8,128)(2,1)S(1)} %select_reduce_fusion), kind=kOutput, calls=%fused_computation.35 | convolution fusion | flops 290455552 | bytes 33031024 | tf_op jit(solution)/shard_map/tj,jrw->trw/dot_general | solution.py:50
  183.9 30.2 %fusion.15 = bf16[8,256,1024]{2,1,0:T(8,128)(2,1)} fusion(bf16[8,256,1024]{2,0,1:T(8,128)(2,1)} %fusion.18, s32[1024]{0:T(1024)S(1)} %multiply_add_fusion.1, pred[1024]{0:T(1024)(128)(4,1)S(1)} %iota_compare_fusion.1), kind=kOutput, calls=%fused_computation.34 | convolution fusion | flops 4315938816 | bytes 8393728 | tf_op jit(solution)/shard_map/frw,kw->frk/dot_general | solution.py:56
  214.1 7.0 %copy.18 = bf16[8,256,1024]{1,0,2:T(8,128)(2,1)} copy(bf16[8,256,1024]{2,1,0:T(8,128)(2,1)} %fusion.15) | data formatting | bytes 8388608 | tf_op jit(solution)/shard_map/convert_element_type | solution.py:58
  221.1 5.0 all-to-all-start
  227.4 52.1 %all-to-all-done = bf16[8,256,1024]{1,0,2:T(8,128)(2,1)} async-done(((bf16[8,256,1024]{1,0,2:T(8,128)(2,1)}), bf16[8,256,1024]{1,0,2:T(8,128)(2,1)}, u32[]{:S(2)}, u32[]{:S(2)}) %all-to-all-start) | async-done | bytes 4194336 | tf_op jit(solution)/shard_map/all_to_all | solution.py:55
  279.5 7.4 %copy.33 = bf16[8,256,4,256]{1,2,3,0:T(4,128)(2,1)} copy(bf16[8,256,4,256]{1,0,3,2:T(8,128)(2,1)} %bitcast.2) | data formatting | bytes 8388608 | tf_op jit(solution)/shard_map/all_to_all | solution.py:55
  286.9 7.8 %all_to_all.29 = bf16[8,1024,256]{1,2,0:T(8,128)(2,1)} reshape(bf16[8,4,256,256]{2,1,3,0:T(4,128)(2,1)} %bitcast.37) | data formatting | bytes 8388608 | tf_op jit(solution)/shard_map/all_to_all | solution.py:55
  294.7 23.9 %convolution_bitcast_fusion = f32[8,1024,256]{1,2,0:T(8,128)} fusion(bf16[8,1024,256]{1,2,0:T(8,128)(2,1)} %all_to_all.29, s32[1024]{0:T(1024)S(1)} %multiply_add_fusion.1, pred[1024]{0:T(1024)(128)(4,1)S(1)} %iota_compare_fusion.1), kind=kOutput, calls=%fused_computation.33 | convolution fusion | flops 4313841664 | bytes 12588032 | tf_op jit(solution)/shard_map/kr,frc->fkc/dot_general | solution.py:52
  318.6 69.1 %while.28 = (s32[]{:T(128)}, f32[1024,256]{1,0:T(8,128)S(1)}, f32[1024,256]{1,0:T(8,128)S(1)}, f32[8,1024,256]{2,1,0:T(8,128)}, f32[8,1024,256]{2,1,0:T(8,128)},...) while((s32[]{:T(128)}, f32[1024,256]{1,0:T(8,128)S(1)}, ...), condition=%wide.region_2.3_spmd.clone, body=%wide.region_1.2_spmd.clone.sunk | while | flops 1572867 | bytes 12584063 | solution.py:78
  387.7 52.3 %while.27 = (s32[]{:T(128)}, f32[1024,256]{1,0:T(8,128)S(1)}, f32[1024,256]{1,0:T(8,128)S(1)}, f32[1024,256]{1,0:T(8,128)S(1)}, s32[]{:T(128)}) while((s32[]{:T(128)}, f32[1024,256]{1,0:T(8,128)S(1)}, f32[1024,256]{1,0:T(8,128)S(1)}, f32[1024,256]{1,0:T(8,128)S(1)}, s32[]{:T(128)}) %tuple.47), condition=%wide.region_4.5_spmd, body=%wide.region_3.4_spmd.sunk | while | flops 524290 | bytes 8388709 | solution.py:85
  392.8 12.0 %collective-permute-done = f32[1024,256]{1,0:T(8,128)S(1)} collective-permute-done((f32[1024,256]{1,0:T(8,128)}, f32[1024,256]{1,0:T(8,128)S(1)}, u32[]{:S(2)}, u32[]{:S(2)}) %collective-permute-start) | collective-permute-done | bytes 1048608 | tf_op jit(solution)/shard_map/while/body/eval_jaxpr/ppermute | solution.py:10
  410.3 12.0 %collective-permute-done = f32[1024,256]{1,0:T(8,128)S(1)} collective-permute-done((f32[1024,256]{1,0:T(8,128)}, f32[1024,256]{1,0:T(8,128)S(1)}, u32[]{:S(2)}, u32[]{:S(2)}) %collective-permute-start) | collective-permute-done | bytes 1048608 | tf_op jit(solution)/shard_map/while/body/eval_jaxpr/ppermute | solution.py:10
  427.8 12.0 %collective-permute-done = f32[1024,256]{1,0:T(8,128)S(1)} collective-permute-done((f32[1024,256]{1,0:T(8,128)}, f32[1024,256]{1,0:T(8,128)S(1)}, u32[]{:S(2)}, u32[]{:S(2)}) %collective-permute-start) | collective-permute-done | bytes 1048608 | tf_op jit(solution)/shard_map/while/body/eval_jaxpr/ppermute | solution.py:10
  440.0 27.7 %convert_bitcast_fusion = bf16[8,1024,256]{1,2,0:T(8,128)(2,1)} fusion(f32[8,1024,256]{2,1,0:T(8,128)} %get-tuple-element.72, f32[8,1024,256]{2,1,0:T(8,128)} %get-tuple-element.73, f32[1024,256]{1,0:T(8,128)S(1)} %get-tuple-element.76, s32[1024]{0:T(1024)S(1)} %multiply_add_fusion.1, pred[1024]{0:T(1024)(128)(4,1)S(1)} %iota_compare_fusion.1), kind=kOutput, calls=%fused_computation.27 | convolution fusion | flops 4322230272 | bytes 22025216 | tf_op jit(solution)/shard_map/kr,fkc->frc/dot_general | solution.py:90
  467.6 6.9 %copy.22 = bf16[8,1024,256]{2,0,1:T(8,128)(2,1)} copy(bf16[8,1024,256]{1,2,0:T(8,128)(2,1)} %convert_bitcast_fusion) | data formatting | bytes 8388608 | tf_op jit(solution)/shard_map/convert_element_type | solution.py:90
  474.6 86.2 %all_to_all.36 = bf16[8,1024,256]{2,0,1:T(8,128)(2,1)S(1)} all-to-all(bf16[8,1024,256]{2,0,1:T(8,128)(2,1)} %copy.22), channel_id=1, replica_groups=mesh['grp'=2,'tm'=4,'tile'=4] {'tile'}, dimensions={1} | all-to-all | bytes 8388608 | tf_op jit(solution)/shard_map/all_to_all | solution.py:89
  560.7 5.2 copy.32
  566.0 7.7 %all_to_all.33 = bf16[8,256,1024]{2,1,0:T(8,128)(2,1)} reshape(bf16[8,256,4,256]{3,2,1,0:T(4,128)(2,1)} %bitcast.39) | data formatting | bytes 8388608 | tf_op jit(solution)/shard_map/all_to_all | solution.py:89
  573.7 22.5 %convolution_convert_fusion = bf16[8,256,1024]{2,1,0:T(8,128)(2,1)} fusion(bf16[8,256,1024]{2,1,0:T(8,128)(2,1)} %all_to_all.33, s32[1024]{0:T(1024)S(1)} %multiply_add_fusion.1, pred[1024]{0:T(1024)(128)(4,1)S(1)} %iota_compare_fusion.1), kind=kOutput, calls=%fused_computation.36 | convolution fusion | flops 4315938816 | bytes 8393728 | tf_op jit(solution)/shard_map/frk,kw->frw/dot_general | solution.py:87
  (63 shorter events, 99.8 us)
Async XLA Ops:
  0.0 108.8 %copy-start.2 = (f32[48]{0:T(128)S(1)}, f32[48]{0:T(128)}, u32[]{:S(2)}) copy-start(f32[48]{0:T(128)} %param.9) | copy-start | bytes 580
  4.5 149.6 %copy-start = (bf16[8,256,1024]{2,0,1:T(8,128)(2,1)}, bf16[8,256,1024]{2,0,1:T(8,128)(2,1)S(1)}, u32[]{:S(2)}) copy-start(bf16[8,256,1024]{2,0,1:T(8,128)(2,1)S(1)} %copy.15) | copy-start | bytes 12582916
  4.5 50.0 %collective-permute-start.1 = (bf16[8,256,1024]{2,0,1:T(8,128)(2,1)S(1)}, bf16[8,256,1024]{2,0,1:T(8,128)(2,1)S(1)}, u32[]{:S(2)}, u32[]{:S(2)}) collective-permute-start(bf16[8,256,1024]{2,0,1:T(8,128)(2,1)S(1)} %copy.15), channel_id=1, source_target_pairs={{0,4},{4,8},{8,12},{1,5},{5,9},{9,13},{2,6},{6,10},{10,14},{3,7},{... | collective-permute-start | bytes 12582920 | tf_op jit(solution)/shard_map/ppermute | solution.py:10
  54.5 49.8 %collective-permute-start.2 = (bf16[8,256,1024]{2,0,1:T(8,128)(2,1)S(1)}, bf16[8,256,1024]{2,0,1:T(8,128)(2,1)S(1)}, u32[]{:S(2)}, u32[]{:S(2)}) collective-permute-start(bf16[8,256,1024]{2,0,1:T(8,128)(2,1)S(1)} %collective-permute-done.1), channel_id=1, source_target_pairs={{0,4},{4,8},{8,12},{1,5},{5,9},{9,13},{2,6},{6,10},{10,14},{3,7},{... | collective-permute-start | bytes 12582920 | tf_op jit(solution)/shard_map/ppermute | solution.py:10
  104.3 49.8 %collective-permute-start.3 = (bf16[8,256,1024]{2,0,1:T(8,128)(2,1)S(1)}, bf16[8,256,1024]{2,0,1:T(8,128)(2,1)S(1)}, u32[]{:S(2)}, u32[]{:S(2)}) collective-permute-start(bf16[8,256,1024]{2,0,1:T(8,128)(2,1)S(1)} %collective-permute-done.2), channel_id=1, source_target_pairs={{0,4},{4,8},{8,12},{1,5},{5,9},{9,13},{2,6},{6,10},{10,14},{3,7},{... | collective-permute-start | bytes 12582920 | tf_op jit(solution)/shard_map/ppermute | solution.py:10
  221.1 5.0 copy-start.1
  221.1 58.3 %all-to-all-start = ((bf16[8,256,1024]{1,0,2:T(8,128)(2,1)}), bf16[8,256,1024]{1,0,2:T(8,128)(2,1)}, u32[]{:S(2)}, u32[]{:S(2)}) async-start(bf16[8,256,1024]{1,0,2:T(8,128)(2,1)} %copy.18), calls=%async_computation | async-start | bytes 8388608 | tf_op jit(solution)/shard_map/all_to_all | solution.py:55
  294.7 23.9 %copy-start.3 = (f32[8]{0:T(128)S(1)}, f32[8]{0:T(128)}, u32[]{:S(2)}) copy-start(f32[8]{0:T(128)} %param.11) | copy-start | bytes 100
  388.9 15.9 %collective-permute-start = (f32[1024,256]{1,0:T(8,128)}, f32[1024,256]{1,0:T(8,128)S(1)}, u32[]{:S(2)}, u32[]{:S(2)}) collective-permute-start(f32[1024,256]{1,0:T(8,128)} %multiply_add_fusion.3), channel_id=1, source_target_pairs={{0,4},{4,8},{8,12},{1,5},{5,9},{9,13},{2,6},{6,10},{10,14},{3,7},{... | collective-permute-start | bytes 3145736 | tf_op jit(solution)/shard_map/while/body/eval_jaxpr/ppermute | solution.py:10
  406.0 16.3 %collective-permute-start = (f32[1024,256]{1,0:T(8,128)}, f32[1024,256]{1,0:T(8,128)S(1)}, u32[]{:S(2)}, u32[]{:S(2)}) collective-permute-start(f32[1024,256]{1,0:T(8,128)} %multiply_add_fusion.3), channel_id=1, source_target_pairs={{0,4},{4,8},{8,12},{1,5},{5,9},{9,13},{2,6},{6,10},{10,14},{3,7},{... | collective-permute-start | bytes 3145736 | tf_op jit(solution)/shard_map/while/body/eval_jaxpr/ppermute | solution.py:10
  423.5 16.3 %collective-permute-start = (f32[1024,256]{1,0:T(8,128)}, f32[1024,256]{1,0:T(8,128)S(1)}, u32[]{:S(2)}, u32[]{:S(2)}) collective-permute-start(f32[1024,256]{1,0:T(8,128)} %multiply_add_fusion.3), channel_id=1, source_target_pairs={{0,4},{4,8},{8,12},{1,5},{5,9},{9,13},{2,6},{6,10},{10,14},{3,7},{... | collective-permute-start | bytes 3145736 | tf_op jit(solution)/shard_map/while/body/eval_jaxpr/ppermute | solution.py:10
where the time goes:
time: 605 us; the launch traced here: 597 us
  waiting for transfers between devices  224 us (37%)
  matrix products  119 us (20%)
  blocking collectives  86.2 us (14%)
  local copies, waits for them, and re-layouts  82.4 us (14%)
  other arithmetic  53.2 us (9%)
  starting transfers between devices  30.7 us (5%)
    ppermute x6, waiting for transfers between devices, from_behind(): return lax.ppermute(block, axis, route)  172 us
    all_to_all x1, blocking collectives, on_device(): lax.all_to_all(jnp.einsum('kr,fkc->frc', basis, running_b, preferred_elem...  86.2 us
    all_to_all x1, waiting for transfers between devices, on_device(): lax.all_to_all(jnp.einsum('frw,kw->frk', wall_heat_flux, basis, preferred...  52.1 us
    dynamic_slice x24, local copies, waits for them, and re-layouts, on_device(): lax.scan(advance, (start_decay, start_state), (spectra, frame_factor))  35.6 us
    dynamic_update_slice x8, other arithmetic, on_device(): lax.scan(advance, (start_decay, start_state), (spectra, frame_factor))  33.4 us
    dot_general x1, matrix products, on_device(): jnp.einsum('frw,kw->frk', wall_heat_flux, basis, preferred_element_type=j...  30.2 us
    dot_general x1, matrix products, on_device(): jnp.einsum('kr,fkc->frc', basis, running_b, preferred_element_type=jnp.fl...  27.7 us
    ppermute x6, starting transfers between devices, from_behind(): return lax.ppermute(block, axis, route)  25.7 us
  transfers between devices with their start and end apart: 7, of which 7 were waited for; matrix products, arithmetic and copies ran while one was open for 0% of the time, Pallas kernels for 0%

commit v1 on v0

--- a/solution.py
+++ b/solution.py
@@ -86,14 +86,22 @@
     running_b = (partial_value + decays * carried[None]).astype(jnp.bfloat16)
     return jnp.einsum(
         "frk,kw->frw",
-        lax.all_to_all(
-            jnp.einsum("kr,fkc->frc", basis, running_b, preferred_element_type=jnp.float32).astype(
-                jnp.bfloat16
+        jnp.concatenate(
+            lax.all_to_all(
+                jnp.stack(
+                    jnp.split(
+                        jnp.einsum(
+                            "kr,fkc->frc", basis, running_b, preferred_element_type=jnp.float32
+                        ).astype(jnp.bfloat16),
+                        lax.axis_size("tile"),
+                        axis=1,
+                    )
+                ),
+                "tile",
+                0,
+                0,
             ),
-            "tile",
-            split_axis=1,
-            concat_axis=2,
-            tiled=True,
+            axis=2,
         ),
         basis,
         preferred_element_type=jnp.float32,

time: 605 us -> 582 us (0.962)
  local copies, waits for them, and re-layouts: 82.4 us -> 63.4 us
    all_to_all x2 -> x0, local copies, waits for them, and re-layouts: 12.9 us -> none  [on_device(): lax.all_to_all(jnp.einsum('kr,fkc->frc', basis, running_b, preferred_elem...]
    convert_element_type x1 -> x0, local copies, waits for them, and re-layouts: 6.94 us -> none  [on_device(): jnp.einsum('kr,fkc->frc', basis, running_b, preferred_element_type=jnp.fl...]
where the time goes in v1:
time: 582 us; the launch traced here: 573 us
  waiting for transfers between devices  224 us (38%)
  matrix products  115 us (20%)
  blocking collectives  85.2 us (15%)
  local copies, waits for them, and re-layouts  63.4 us (11%)
  other arithmetic  53.8 us (9%)
  starting transfers between devices  30.7 us (5%)
    ppermute x6, waiting for transfers between devices, from_behind(): return lax.ppermute(block, axis, route)  172 us
    all_to_all x1, blocking collectives, on_device(): lax.all_to_all(jnp.stack(jnp.split(jnp.einsum('kr,fkc->frc', basis, runni...  85.2 us
    all_to_all x1, waiting for transfers between devices, on_device(): lax.all_to_all(jnp.einsum('frw,kw->frk', wall_heat_flux, basis, preferred...  52.1 us
    dynamic_slice x24, local copies, waits for them, and re-layouts, on_device(): lax.scan(advance, (start_decay, start_state), (spectra, frame_factor))  35.6 us
    dynamic_update_slice x8, other arithmetic, on_device(): lax.scan(advance, (start_decay, start_state), (spectra, frame_factor))  33.4 us
    dot_general x1, matrix products, on_device(): jnp.einsum('frw,kw->frk', wall_heat_flux, basis, preferred_element_type=j...  30.2 us
    ppermute x6, starting transfers between devices, from_behind(): return lax.ppermute(block, axis, route)  25.7 us
    dot_general x1, matrix products, on_device(): jnp.einsum('kr,fkc->frc', basis, running_b, preferred_element_type=jnp.fl...  25.6 us
  transfers between devices with their start and end apart: 7, of which 7 were waited for; matrix products, arithmetic and copies ran while one was open for 0% of the time, Pallas kernels for 0%

profile of v1, /device:TPU:1, one launch (start us, length us, event | category | flops | bytes accessed | tf_op | source)
XLA Modules:
  0.0 573.5 jit_solution(5446612645143857947)
XLA Ops:
  0.0 4.5 copy.22
  4.5 4.5 collective-permute-start.1
  9.1 45.4 %collective-permute-done.1 = bf16[8,256,1024]{2,0,1:T(8,128)(2,1)S(1)} collective-permute-done((bf16[8,256,1024]{2,0,1:T(8,128)(2,1)S(1)}, bf16[8,256,1024]{2,0,1:T(8,128)(2,1)S(1)}, u32[]{:S(2)}, u32[]{:S(2)}) %collective-permute-start.1) | collective-permute-done | bytes 4194336 | tf_op jit(solution)/shard_map/ppermute | solution.py:10
  54.5 4.4 collective-permute-start.2
  58.9 45.4 %collective-permute-done.2 = bf16[8,256,1024]{2,0,1:T(8,128)(2,1)S(1)} collective-permute-done((bf16[8,256,1024]{2,0,1:T(8,128)(2,1)S(1)}, bf16[8,256,1024]{2,0,1:T(8,128)(2,1)S(1)}, u32[]{:S(2)}, u32[]{:S(2)}) %collective-permute-start.2) | collective-permute-done | bytes 4194336 | tf_op jit(solution)/shard_map/ppermute | solution.py:10
  104.3 4.4 collective-permute-start.3
  109.0 45.1 %collective-permute-done.3 = bf16[8,256,1024]{2,0,1:T(8,128)(2,1)S(1)} collective-permute-done((bf16[8,256,1024]{2,0,1:T(8,128)(2,1)S(1)}, bf16[8,256,1024]{2,0,1:T(8,128)(2,1)S(1)}, u32[]{:S(2)}, u32[]{:S(2)}) %collective-permute-start.3) | collective-permute-done | bytes 4194336 | tf_op jit(solution)/shard_map/ppermute | solution.py:10
  154.1 14.9 %pad_maximum_fusion = bf16[47,256,1024]{2,0,1:T(8,128)(2,1)} fusion(bf16[8,256,1024]{2,0,1:T(8,128)(2,1)S(1)} %collective-permute-done.1, bf16[8,256,1024]{2,0,1:T(8,128)(2,1)S(1)} %collective-permute-done.2, bf16[8,256,1024]{2,0,1:T(8,128)(2,1)S(1)} %collective-permute-done.3, bf16[47]{0:T(256)(128)(2,1)S(1)} %pad_slice_fusion), kind=kLoop, calls=%fused_computation.11 | loop fusion | flops 98566144 | bytes 37224544 | tf_op jit(solution)/shard_map/concatenate | solution.py:47
  169.0 14.9 %fusion.18 = bf16[8,256,1024]{2,0,1:T(8,128)(2,1)} fusion(bf16[8,256,1024]{2,0,1:T(8,128)(2,1)} %copy-done, bf16[47,256,1024]{2,0,1:T(8,128)(2,1)} %pad_maximum_fusion, bf16[8,55]{1,0:T(8,128)(2,1)S(1)} %select_reduce_fusion), kind=kOutput, calls=%fused_computation.35 | convolution fusion | flops 290455552 | bytes 33031024 | tf_op jit(solution)/shard_map/tj,jrw->trw/dot_general | solution.py:50
  183.9 30.2 %fusion.15 = bf16[8,256,1024]{2,1,0:T(8,128)(2,1)} fusion(bf16[8,256,1024]{2,0,1:T(8,128)(2,1)} %fusion.18, s32[1024]{0:T(1024)S(1)} %multiply_add_fusion.1, pred[1024]{0:T(1024)(128)(4,1)S(1)} %iota_compare_fusion.1), kind=kOutput, calls=%fused_computation.34 | convolution fusion | flops 4315938816 | bytes 8393728 | tf_op jit(solution)/shard_map/frw,kw->frk/dot_general | solution.py:56
  214.1 7.0 %copy.25 = bf16[8,256,1024]{1,0,2:T(8,128)(2,1)} copy(bf16[8,256,1024]{2,1,0:T(8,128)(2,1)} %fusion.15) | data formatting | bytes 8388608 | tf_op jit(solution)/shard_map/convert_element_type | solution.py:58
  221.1 5.0 all-to-all-start
  227.4 52.1 %all-to-all-done = bf16[8,256,1024]{1,0,2:T(8,128)(2,1)} async-done(((bf16[8,256,1024]{1,0,2:T(8,128)(2,1)}), bf16[8,256,1024]{1,0,2:T(8,128)(2,1)}, u32[]{:S(2)}, u32[]{:S(2)}) %all-to-all-start) | async-done | bytes 4194336 | tf_op jit(solution)/shard_map/all_to_all | solution.py:55
  279.5 7.4 %copy.39 = bf16[8,256,4,256]{1,2,3,0:T(4,128)(2,1)} copy(bf16[8,256,4,256]{1,0,3,2:T(8,128)(2,1)} %bitcast.2) | data formatting | bytes 8388608 | tf_op jit(solution)/shard_map/all_to_all | solution.py:55
  286.9 7.8 %all_to_all.19 = bf16[8,1024,256]{1,2,0:T(8,128)(2,1)} reshape(bf16[8,4,256,256]{2,1,3,0:T(4,128)(2,1)} %bitcast.43) | data formatting | bytes 8388608 | tf_op jit(solution)/shard_map/all_to_all | solution.py:55
  294.7 23.8 %convolution_bitcast_fusion = f32[8,1024,256]{1,2,0:T(8,128)} fusion(bf16[8,1024,256]{1,2,0:T(8,128)(2,1)} %all_to_all.19, s32[1024]{0:T(1024)S(1)} %multiply_add_fusion.1, pred[1024]{0:T(1024)(128)(4,1)S(1)} %iota_compare_fusion.1), kind=kOutput, calls=%fused_computation.33 | convolution fusion | flops 4313841664 | bytes 12588032 | tf_op jit(solution)/shard_map/kr,frc->fkc/dot_general | solution.py:52
  318.5 69.0 %while.28 = (s32[]{:T(128)}, f32[1024,256]{1,0:T(8,128)S(1)}, f32[1024,256]{1,0:T(8,128)S(1)}, f32[8,1024,256]{2,1,0:T(8,128)}, f32[8,1024,256]{2,1,0:T(8,128)},...) while((s32[]{:T(128)}, f32[1024,256]{1,0:T(8,128)S(1)}, ...), condition=%wide.region_2.3_spmd.clone, body=%wide.region_1.2_spmd.clone.sunk | while | flops 1572867 | bytes 12584063 | solution.py:78
  387.6 52.3 %while.27 = (s32[]{:T(128)}, f32[1024,256]{1,0:T(8,128)S(1)}, f32[1024,256]{1,0:T(8,128)S(1)}, f32[1024,256]{1,0:T(8,128)S(1)}, s32[]{:T(128)}) while((s32[]{:T(128)}, f32[1024,256]{1,0:T(8,128)S(1)}, f32[1024,256]{1,0:T(8,128)S(1)}, f32[1024,256]{1,0:T(8,128)S(1)}, s32[]{:T(128)}) %tuple.51), condition=%wide.region_4.5_spmd, body=%wide.region_3.4_spmd.sunk | while | flops 524290 | bytes 8388709 | solution.py:85
  392.7 12.0 %collective-permute-done = f32[1024,256]{1,0:T(8,128)S(1)} collective-permute-done((f32[1024,256]{1,0:T(8,128)}, f32[1024,256]{1,0:T(8,128)S(1)}, u32[]{:S(2)}, u32[]{:S(2)}) %collective-permute-start) | collective-permute-done | bytes 1048608 | tf_op jit(solution)/shard_map/while/body/eval_jaxpr/ppermute | solution.py:10
  410.2 12.0 %collective-permute-done = f32[1024,256]{1,0:T(8,128)S(1)} collective-permute-done((f32[1024,256]{1,0:T(8,128)}, f32[1024,256]{1,0:T(8,128)S(1)}, u32[]{:S(2)}, u32[]{:S(2)}) %collective-permute-start) | collective-permute-done | bytes 1048608 | tf_op jit(solution)/shard_map/while/body/eval_jaxpr/ppermute | solution.py:10
  427.7 12.0 %collective-permute-done = f32[1024,256]{1,0:T(8,128)S(1)} collective-permute-done((f32[1024,256]{1,0:T(8,128)}, f32[1024,256]{1,0:T(8,128)S(1)}, u32[]{:S(2)}, u32[]{:S(2)}) %collective-permute-start) | collective-permute-done | bytes 1048608 | tf_op jit(solution)/shard_map/while/body/eval_jaxpr/ppermute | solution.py:10
  439.9 25.6 %convert_bitcast_fusion = bf16[8,1024,256]{1,2,0:T(8,128)(2,1)S(1)} fusion(f32[8,1024,256]{2,1,0:T(8,128)} %get-tuple-element.72, f32[8,1024,256]{2,1,0:T(8,128)} %get-tuple-element.73, f32[1024,256]{1,0:T(8,128)S(1)} %get-tuple-element.76, s32[1024]{0:T(1024)S(1)} %multiply_add_fusion.1, pred[1024]{0:T(1024)(128)(4,1)S(1)} %iota_compare_fusion.1), kind=kOutput, calls=%fused_computation.27 | convolution fusion | flops 4322230272 | bytes 22025216 | tf_op jit(solution)/shard_map/kr,fkc->frc/dot_general | solution.py:93
  466.6 85.2 %all_to_all.23 = bf16[4,8,256,256]{2,3,1,0:T(8,128)(2,1)S(1)} all-to-all(bf16[4,8,256,256]{2,3,1,0:T(8,128)(2,1)S(1)} %pad_maximum_fusion.3), channel_id=1, replica_groups=mesh['grp'=2,'tm'=4,'tile'=4] {'tile'}, dimensions={0} | all-to-all | bytes 8388608 | tf_op jit(solution)/shard_map/all_to_all | solution.py:90
  552.3 20.8 %convolution_convert_fusion = bf16[8,256,1024]{2,1,0:T(8,128)(2,1)} fusion(bf16[8,256,1024]{1,2,0:T(8,128)(2,1)S(1)} %bitcast.45, s32[1024]{0:T(1024)S(1)} %multiply_add_fusion.1, pred[1024]{0:T(1024)(128)(4,1)S(1)} %iota_compare_fusion.1), kind=kOutput, calls=%fused_computation.36 | convolution fusion | flops 4315938816 | bytes 8393728 | tf_op jit(solution)/shard_map/frk,kw->frw/dot_general | solution.py:87
  (63 shorter events, 88.0 us)
Async XLA Ops:
  0.0 108.8 %copy-start.2 = (f32[48]{0:T(128)S(1)}, f32[48]{0:T(128)}, u32[]{:S(2)}) copy-start(f32[48]{0:T(128)} %param.9) | copy-start | bytes 580
  4.5 149.6 %copy-start = (bf16[8,256,1024]{2,0,1:T(8,128)(2,1)}, bf16[8,256,1024]{2,0,1:T(8,128)(2,1)S(1)}, u32[]{:S(2)}) copy-start(bf16[8,256,1024]{2,0,1:T(8,128)(2,1)S(1)} %copy.22) | copy-start | bytes 12582916
  4.5 50.0 %collective-permute-start.1 = (bf16[8,256,1024]{2,0,1:T(8,128)(2,1)S(1)}, bf16[8,256,1024]{2,0,1:T(8,128)(2,1)S(1)}, u32[]{:S(2)}, u32[]{:S(2)}) collective-permute-start(bf16[8,256,1024]{2,0,1:T(8,128)(2,1)S(1)} %copy.22), channel_id=1, source_target_pairs={{0,4},{4,8},{8,12},{1,5},{5,9},{9,13},{2,6},{6,10},{10,14},{3,7},{... | collective-permute-start | bytes 12582920 | tf_op jit(solution)/shard_map/ppermute | solution.py:10
  54.5 49.8 %collective-permute-start.2 = (bf16[8,256,1024]{2,0,1:T(8,128)(2,1)S(1)}, bf16[8,256,1024]{2,0,1:T(8,128)(2,1)S(1)}, u32[]{:S(2)}, u32[]{:S(2)}) collective-permute-start(bf16[8,256,1024]{2,0,1:T(8,128)(2,1)S(1)} %collective-permute-done.1), channel_id=1, source_target_pairs={{0,4},{4,8},{8,12},{1,5},{5,9},{9,13},{2,6},{6,10},{10,14},{3,7},{... | collective-permute-start | bytes 12582920 | tf_op jit(solution)/shard_map/ppermute | solution.py:10
  104.3 49.8 %collective-permute-start.3 = (bf16[8,256,1024]{2,0,1:T(8,128)(2,1)S(1)}, bf16[8,256,1024]{2,0,1:T(8,128)(2,1)S(1)}, u32[]{:S(2)}, u32[]{:S(2)}) collective-permute-start(bf16[8,256,1024]{2,0,1:T(8,128)(2,1)S(1)} %collective-permute-done.2), channel_id=1, source_target_pairs={{0,4},{4,8},{8,12},{1,5},{5,9},{9,13},{2,6},{6,10},{10,14},{3,7},{... | collective-permute-start | bytes 12582920 | tf_op jit(solution)/shard_map/ppermute | solution.py:10
  221.1 5.0 copy-start.1
  221.1 58.3 %all-to-all-start = ((bf16[8,256,1024]{1,0,2:T(8,128)(2,1)}), bf16[8,256,1024]{1,0,2:T(8,128)(2,1)}, u32[]{:S(2)}, u32[]{:S(2)}) async-start(bf16[8,256,1024]{1,0,2:T(8,128)(2,1)} %copy.25), calls=%async_computation | async-start | bytes 8388608 | tf_op jit(solution)/shard_map/all_to_all | solution.py:55
  294.7 23.8 %copy-start.3 = (f32[8]{0:T(128)S(1)}, f32[8]{0:T(128)}, u32[]{:S(2)}) copy-start(f32[8]{0:T(128)} %param.11) | copy-start | bytes 100
  388.8 16.0 %collective-permute-start = (f32[1024,256]{1,0:T(8,128)}, f32[1024,256]{1,0:T(8,128)S(1)}, u32[]{:S(2)}, u32[]{:S(2)}) collective-permute-start(f32[1024,256]{1,0:T(8,128)} %multiply_add_fusion.3), channel_id=1, source_target_pairs={{0,4},{4,8},{8,12},{1,5},{5,9},{9,13},{2,6},{6,10},{10,14},{3,7},{... | collective-permute-start | bytes 3145736 | tf_op jit(solution)/shard_map/while/body/eval_jaxpr/ppermute | solution.py:10
  405.9 16.3 %collective-permute-start = (f32[1024,256]{1,0:T(8,128)}, f32[1024,256]{1,0:T(8,128)S(1)}, u32[]{:S(2)}, u32[]{:S(2)}) collective-permute-start(f32[1024,256]{1,0:T(8,128)} %multiply_add_fusion.3), channel_id=1, source_target_pairs={{0,4},{4,8},{8,12},{1,5},{5,9},{9,13},{2,6},{6,10},{10,14},{3,7},{... | collective-permute-start | bytes 3145736 | tf_op jit(solution)/shard_map/while/body/eval_jaxpr/ppermute | solution.py:10
  423.4 16.3 %collective-permute-start = (f32[1024,256]{1,0:T(8,128)}, f32[1024,256]{1,0:T(8,128)S(1)}, u32[]{:S(2)}, u32[]{:S(2)}) collective-permute-start(f32[1024,256]{1,0:T(8,128)} %multiply_add_fusion.3), channel_id=1, source_target_pairs={{0,4},{4,8},{8,12},{1,5},{5,9},{9,13},{2,6},{6,10},{10,14},{3,7},{... | collective-permute-start | bytes 3145736 | tf_op jit(solution)/shard_map/while/body/eval_jaxpr/ppermute | solution.py:10
